TPU v7x, 128 devices: a whole 4x4x4 slice. The times are simulated.
128 devices in a mesh: row: 8 (over y, core), col: 16 (over x, z).
Axes of the slice: x: 4, y: 4, z: 4, core: 2. Of those that a mesh axis runs over, the one named last changes fastest.
Arguments:
- scores: float32 [32, 98304], P(None, ('row', 'col')), may hold values from -60 to 60
- tile_values: bfloat16 [8, 16, 480, 128, 128], P('row', 'col'), may hold values from 0 to 1
- tile_rows: int32 [8, 16, 480], P('row', 'col'), may hold values from 0 to 95, as said below
- tile_cols: int32 [8, 16, 480], P('row', 'col'), may hold values from 0 to 47, as said below
- tile_count: int32 [8, 16], P('row', 'col'), may hold values from 240 to 480, as said below
Outputs:
- solution: float32 [32, 98304], P(None, ('row', 'col'))
- residual: float32 [32, 98304], P(None, ('row', 'col'))
Inputs may be any that keep to these rules, and one draw needn't show every extreme that they name: `tile_rows`: on every device each local row tile is named by exactly 5 of the 480 slots. `tile_cols`: on every device each local column tile is named by exactly 10 of the slots. Only the first tile_count slots of a device are live; some device has all 480 slots live.
All inputs are finite; a program needn't handle non-finite values.
Results may differ from a plain program's by a relative error of at most 0.0031.
Values may be sent and summed in bfloat16 or wider, within the bound.
A program may use at most 128 MiB of HBM per device.

v0:
```python
import jax
import jax.numpy as jnp
from jax import lax
from jax.sharding import PartitionSpec as P

PER_ROW = 5
ITERS = 3
coupling = 0.2


def per_device(scores, tile_values, tile_rows, tile_cols, tile_count):
    tile_blocks = tile_values[0, 0]
    row_tile_ids = tile_rows[0, 0]
    col_tile_ids = tile_cols[0, 0]
    live_count = tile_count[0, 0]
    slot_count = tile_blocks.shape[0]
    tile_size = tile_blocks.shape[1]
    task_count = scores.shape[0]
    piece_len = scores.shape[1]
    row_span = piece_len * lax.axis_size("col")
    col_span = piece_len * lax.axis_size("row")
    row_tiles = row_span // tile_size
    col_tiles = col_span // tile_size
    block_slots = slot_count // PER_ROW
    live_mask = (jnp.arange(slot_count, dtype=jnp.int32) < live_count).astype(jnp.float32)
    row_weight = jnp.sum(tile_blocks, axis=2, dtype=jnp.float32) * live_mask[:, None]
    col_weight = jnp.sum(tile_blocks, axis=1, dtype=jnp.float32) * live_mask[:, None]
    row_degree_part = (
        jnp.zeros((row_tiles, tile_size), jnp.float32)
        .at[row_tile_ids]
        .add(row_weight)
        .reshape(1, row_span)
    )
    col_degree_part = (
        jnp.zeros((col_tiles, tile_size), jnp.float32)
        .at[col_tile_ids]
        .add(col_weight)
        .reshape(1, col_span)
    )

    def to_rows(partial_value):
        return lax.psum_scatter(partial_value, "col", scatter_dimension=1, tiled=True)

    def to_cols(partial_value):
        return lax.psum_scatter(partial_value, "row", scatter_dimension=1, tiled=True)

    degree = 0.5 * (to_rows(row_degree_part) + to_cols(col_degree_part))

    def inner_sums(parts):
        return lax.psum(parts, ("row", "col"))

    solution = jnp.zeros_like(scores)
    residual = scores
    direction = scores
    norm_now = inner_sums(jnp.sum(residual * residual, axis=1))
    for step_index in range(ITERS):
        graph_own_low = direction.astype(jnp.bfloat16)
        graph_col_dir = lax.all_gather(graph_own_low, "row", axis=1, tiled=True)
        graph_row_dir = lax.all_gather(graph_own_low, "col", axis=1, tiled=True)
        col_blocks = graph_col_dir.reshape(task_count, col_tiles, tile_size)
        row_blocks = graph_row_dir.reshape(task_count, row_tiles, tile_size)
        block_count = (live_count + block_slots - 1) // block_slots

        def one_block(block_index, totals):
            forward_sum, backward_sum = totals
            first_slot = block_index * block_slots
            tiles_here = lax.dynamic_slice_in_dim(tile_blocks, first_slot, block_slots, 0)
            rows_here = lax.dynamic_slice_in_dim(row_tile_ids, first_slot, block_slots, 0)
            cols_here = lax.dynamic_slice_in_dim(col_tile_ids, first_slot, block_slots, 0)
            live_here = (first_slot + jnp.arange(block_slots, dtype=jnp.int32) < live_count).astype(
                jnp.float32
            )
            col_pieces = jnp.take(col_blocks, cols_here, axis=1)
            row_pieces = jnp.take(row_blocks, rows_here, axis=1)
            forward = (
                jnp.einsum(
                    "ksd,sod->kso", col_pieces, tiles_here, preferred_element_type=jnp.float32
                )
                * live_here[None, :, None]
            )
            backward = (
                jnp.einsum(
                    "kso,sod->ksd", row_pieces, tiles_here, preferred_element_type=jnp.float32
                )
                * live_here[None, :, None]
            )
            return (
                forward_sum.at[:, rows_here, :].add(forward),
                backward_sum.at[:, cols_here, :].add(backward),
            )

        empty_sums = (
            jnp.zeros((task_count, row_tiles, tile_size), jnp.float32),
            jnp.zeros((task_count, col_tiles, tile_size), jnp.float32),
        )
        forward_sum, backward_sum = lax.fori_loop(0, block_count, one_block, empty_sums)
        forward_part = forward_sum.reshape(task_count, row_span)
        backward_part = backward_sum.reshape(task_count, col_span)
        image_field = direction + coupling * (
            degree * direction - 0.5 * (to_rows(forward_part) + to_cols(backward_part))
        )
        curvature = inner_sums(jnp.sum(direction * image_field, axis=1))
        step_size = norm_now / curvature
        solution = solution + step_size[:, None] * direction
        residual = residual - step_size[:, None] * image_field
        if step_index + 1 < ITERS:
            norm_next = inner_sums(jnp.sum(residual * residual, axis=1))
            direction = residual + (norm_next / norm_now)[:, None] * direction
            norm_now = norm_next
    return (solution, residual)


def solution(mesh):
    return jax.shard_map(
        per_device,
        mesh=mesh,
        in_specs=(
            P(None, ("row", "col")),
            P("row", "col", None, None, None),
            P("row", "col", None),
            P("row", "col", None),
            P("row", "col"),
        ),
        out_specs=(P(None, ("row", "col")), P(None, ("row", "col"))),
        check_vma=False,
    )
```

profile of v0, /device:TPU:1, one launch (start us, length us, event | category | flops | bytes accessed | tf_op | source)
XLA Modules:
  0.0 1218.0 jit_solution(540083142210740069)
XLA Ops:
  7.9 9.8 convert_reduce_fusion
  26.0 4.0 copy.53
  30.8 23.3 %all_gather.19 = bf16[32,12288]{1,0:T(8,128)(2,1)S(1)} all-gather(bf16[32,768]{1,0:T(8,128)(2,1)S(1)} %convert_element_type.43), channel_id=1, replica_groups=mesh['row'=8,'col'=16] {'col'}, dimensions={1}, use_global_device_ids=true | all-gather | bytes 835584 | tf_op jit(solution)/shard_map/all_gather | solution.py:59
  54.2 17.6 %all_gather.18 = bf16[32,6144]{1,0:T(8,128)(2,1)S(1)} all-gather(bf16[32,768]{1,0:T(8,128)(2,1)S(1)} %convert_element_type.43), channel_id=1, replica_groups=mesh['row'=8,'col'=16] {'row'}, dimensions={1}, use_global_device_ids=true | all-gather | bytes 442368 | tf_op jit(solution)/shard_map/all_gather | solution.py:58
  74.4 137.2 %while.36 = (s32[]{:T(128)}, f32[32,96,128]{2,0,1:T(8,128)}, f32[32,48,128]{2,0,1:T(8,128)S(1)}, s32[]{:T(128)}, s32[480]{0:T(512)}, /*index=5*/bf16[480,128,128...) while((s32[]{:T(128)}, f32[32,96,128]{2,0,1:T(8,128)}, ...), condition=%wide.region_11.14_spmd, body=%wide.region_8.13_spmd.sunk | while | flops 203689376 | bytes 23607144 | solution.py:96
  77.1 3.7 multiply_bitcast_fusion.12
  80.8 11.9 scatter_fusion
  97.4 4.4 scatter_fusion.1
  104.6 3.8 multiply_bitcast_fusion.12
  108.4 11.8 scatter_fusion
  125.0 4.5 scatter_fusion.1
  132.2 3.7 multiply_bitcast_fusion.12
  135.9 11.8 scatter_fusion
  152.5 4.4 scatter_fusion.1
  159.6 3.7 multiply_bitcast_fusion.12
  163.3 11.8 scatter_fusion
  179.8 4.4 scatter_fusion.1
  187.0 3.7 multiply_bitcast_fusion.12
  190.6 11.8 scatter_fusion
  207.2 4.4 scatter_fusion.1
  217.0 22.7 %reduce-scatter.15.cloned.1.call-done = f32[32,768]{1,0:T(8,128)} async-done(((f32[32,6144]{1,0:T(8,128)}), f32[32,768]{1,0:T(8,128)}) %reduce-scatter.15.cloned.1.call-update) | async-done | bytes 98320 | tf_op jit(solution)/shard_map/reduce_scatter | solution.py:45
  239.7 77.5 %reduce-scatter.13.cloned.1.call-done = f32[32,768]{1,0:T(8,128)} async-done(((f32[32,12288]{1,0:T(8,128)}), f32[32,768]{1,0:T(8,128)}) %reduce-scatter.13.cloned.1.call-update) | async-done | bytes 98320 | tf_op jit(solution)/shard_map/reduce_scatter | solution.py:42
  318.3 66.1 %all-reduce = (f32[32]{0:T(128)S(1)}, f32[32]{0:T(128)S(1)}) all-reduce(f32[32]{0:T(128)S(1)} %get-tuple-element.255, f32[32]{0:T(128)S(1)} %get-tuple-element.254), channel_id=1, replica_groups=mesh['row'=8,'col'=16] {'row','col'}, use_global_device_ids=true, to_apply=%region_1.0 | all-reduce | flops 64 | bytes 512 | tf_op jit(solution)/shard_map/psum | solution.py:50
  385.5 62.5 %psum.44 = f32[32]{0:T(128)S(1)} all-reduce(f32[32]{0:T(128)S(1)} %get-tuple-element.334), channel_id=1, replica_groups=mesh['row'=8,'col'=16] {'row','col'}, use_global_device_ids=true, to_apply=%region_17.20 | all-reduce | flops 32 | bytes 256 | tf_op jit(solution)/shard_map/psum | solution.py:50
  448.8 19.0 %all_gather.21 = bf16[32,12288]{1,0:T(8,128)(2,1)S(1)} all-gather(bf16[32,768]{1,0:T(8,128)(2,1)S(1)} %get-tuple-element.332), channel_id=1, replica_groups=mesh['row'=8,'col'=16] {'col'}, dimensions={1}, use_global_device_ids=true | all-gather | bytes 835584 | tf_op jit(solution)/shard_map/all_gather | solution.py:59
  467.8 18.5 %all_gather.20 = bf16[32,6144]{1,0:T(8,128)(2,1)S(1)} all-gather(bf16[32,768]{1,0:T(8,128)(2,1)S(1)} %get-tuple-element.332), channel_id=1, replica_groups=mesh['row'=8,'col'=16] {'row'}, dimensions={1}, use_global_device_ids=true | all-gather | bytes 442368 | tf_op jit(solution)/shard_map/all_gather | solution.py:58
  488.9 137.0 %while.37 = (s32[]{:T(128)}, f32[32,96,128]{2,0,1:T(8,128)}, f32[32,48,128]{2,0,1:T(8,128)S(1)}, s32[]{:T(128)}, s32[480]{0:T(512)}, /*index=5*/bf16[480,128,128...) while((s32[]{:T(128)}, f32[32,96,128]{2,0,1:T(8,128)}, ...), condition=%wide.region_21.24_spmd, body=%wide.region_18.23_spmd.sunk | while | flops 203689376 | bytes 23607556 | solution.py:96
  491.6 3.7 multiply_bitcast_fusion.14
  495.3 11.8 scatter_fusion.2
  511.8 4.4 scatter_fusion.3
  519.0 3.7 multiply_bitcast_fusion.14
  522.6 11.8 scatter_fusion.2
  539.2 4.5 scatter_fusion.3
  546.4 3.7 multiply_bitcast_fusion.14
  550.0 11.8 scatter_fusion.2
  566.6 4.4 scatter_fusion.3
  573.7 3.7 multiply_bitcast_fusion.14
  577.4 11.8 scatter_fusion.2
  594.0 4.4 scatter_fusion.3
  601.1 3.7 multiply_bitcast_fusion.14
  604.8 11.8 scatter_fusion.2
  621.4 4.4 scatter_fusion.3
  628.9 23.5 %reduce-scatter.19.cloned.1.call-done = f32[32,768]{1,0:T(8,128)} async-done(((f32[32,6144]{1,0:T(8,128)}), f32[32,768]{1,0:T(8,128)}) %reduce-scatter.19.cloned.1.call-update) | async-done | bytes 98320 | tf_op jit(solution)/shard_map/reduce_scatter | solution.py:45
  652.3 77.6 %reduce-scatter.17.cloned.1.call-done = f32[32,768]{1,0:T(8,128)} async-done(((f32[32,12288]{1,0:T(8,128)}), f32[32,768]{1,0:T(8,128)}) %reduce-scatter.17.cloned.1.call-update) | async-done | bytes 98320 | tf_op jit(solution)/shard_map/reduce_scatter | solution.py:42
  731.0 65.9 %psum.45 = f32[32]{0:T(128)S(1)} all-reduce(f32[32]{0:T(128)S(1)} %multiply_reduce_fusion.2), channel_id=1, replica_groups=mesh['row'=8,'col'=16] {'row','col'}, use_global_device_ids=true, to_apply=%region_25.28 | all-reduce | flops 32 | bytes 256 | tf_op jit(solution)/shard_map/psum | solution.py:50
  798.1 62.5 %psum.46 = f32[32]{0:T(128)S(1)} all-reduce(f32[32]{0:T(128)S(1)} %get-tuple-element.330), channel_id=1, replica_groups=mesh['row'=8,'col'=16] {'row','col'}, use_global_device_ids=true, to_apply=%region_27.30 | all-reduce | flops 32 | bytes 256 | tf_op jit(solution)/shard_map/psum | solution.py:50
  860.7 19.0 %all_gather.23 = bf16[32,12288]{1,0:T(8,128)(2,1)S(1)} all-gather(bf16[32,768]{1,0:T(8,128)(2,1)S(1)} %fusion.69), channel_id=1, replica_groups=mesh['row'=8,'col'=16] {'col'}, dimensions={1}, use_global_device_ids=true | all-gather | bytes 835584 | tf_op jit(solution)/shard_map/all_gather | solution.py:59
  879.7 18.8 %all_gather.22 = bf16[32,6144]{1,0:T(8,128)(2,1)S(1)} all-gather(bf16[32,768]{1,0:T(8,128)(2,1)S(1)} %fusion.69), channel_id=1, replica_groups=mesh['row'=8,'col'=16] {'row'}, dimensions={1}, use_global_device_ids=true | all-gather | bytes 442368 | tf_op jit(solution)/shard_map/all_gather | solution.py:58
  901.0 137.0 %while.38 = (s32[]{:T(128)}, f32[32,96,128]{2,0,1:T(8,128)}, f32[32,48,128]{2,0,1:T(8,128)S(1)}, s32[]{:T(128)}, s32[480]{0:T(512)}, /*index=5*/bf16[480,128,128...) while((s32[]{:T(128)}, f32[32,96,128]{2,0,1:T(8,128)}, ...), condition=%wide.region_31.34_spmd, body=%wide.region_28.33_spmd.sunk | while | flops 203689376 | bytes 23607556 | solution.py:96
  903.7 3.7 multiply_bitcast_fusion.16
  907.4 11.8 scatter_fusion.4
  924.0 4.4 scatter_fusion.5
  934.8 11.8 scatter_fusion.4
  951.3 4.5 scatter_fusion.5
  958.5 3.7 multiply_bitcast_fusion.16
  962.2 11.8 scatter_fusion.4
  978.7 4.4 scatter_fusion.5
  989.6 11.8 scatter_fusion.4
  1006.1 4.4 scatter_fusion.5
  1017.0 11.8 scatter_fusion.4
  1033.5 4.4 scatter_fusion.5
  1041.0 23.5 %reduce-scatter.23.cloned.1.call-done = f32[32,768]{1,0:T(8,128)} async-done(((f32[32,6144]{1,0:T(8,128)}), f32[32,768]{1,0:T(8,128)}) %reduce-scatter.23.cloned.1.call-update) | async-done | bytes 98320 | tf_op jit(solution)/shard_map/reduce_scatter | solution.py:45
  1064.5 77.8 %reduce-scatter.21.cloned.1.call-done = f32[32,768]{1,0:T(8,128)} async-done(((f32[32,12288]{1,0:T(8,128)}), f32[32,768]{1,0:T(8,128)}) %reduce-scatter.21.cloned.1.call-update) | async-done | bytes 98320 | tf_op jit(solution)/shard_map/reduce_scatter | solution.py:42
  1143.4 65.9 %psum.47 = f32[32]{0:T(128)S(1)} all-reduce(f32[32]{0:T(128)S(1)} %multiply_reduce_fusion), channel_id=1, replica_groups=mesh['row'=8,'col'=16] {'row','col'}, use_global_device_ids=true, to_apply=%region_35.38 | all-reduce | flops 32 | bytes 256 | tf_op jit(solution)/shard_map/psum | solution.py:50
  (231 shorter events, 158.3 us)
Async XLA Ops:
  7.2 207.5 %reduce-scatter.27.cloned.1.call-start = ((), (), s32[]{:S(2)}) async-start(), calls=%async_computation.15 | async-start | bytes 3538944
  22.9 192.9 %reduce-scatter.25.cloned.1.call-start = ((), (), s32[]{:S(2)}) async-start(), calls=%async_computation.14 | async-start | bytes 6684672
  29.9 0.9 copy-start.5
  30.0 209.8 %reduce-scatter.15.cloned.1.call-start = ((), (), s32[]{:S(2)}) async-start(), calls=%async_computation.9 | async-start | bytes 884736 | tf_op jit(solution)/shard_map/reduce_scatter | solution.py:45
  211.6 1.7 copy-start.1
  212.6 104.6 %reduce-scatter.13.cloned.1.call-start = ((), (), s32[]{:S(2)}) async-start(), calls=%async_computation.8 | async-start | bytes 1671168 | tf_op jit(solution)/shard_map/reduce_scatter | solution.py:42
  214.6 102.6 %copy-start.6 = (f32[32,768]{1,0:T(8,128)S(1)}, f32[32,768]{1,0:T(8,128)}, u32[]{:S(2)}) copy-start(f32[32,768]{1,0:T(8,128)} %param.15) | copy-start | bytes 294916
  214.6 437.7 %reduce-scatter.19.cloned.1.call-start = ((), (), s32[]{:S(2)}) async-start(), calls=%async_computation.11 | async-start | bytes 884736 | tf_op jit(solution)/shard_map/reduce_scatter | solution.py:45
  384.4 103.0 %copy-start.16 = (f32[32]{0:T(128)}, f32[32]{0:T(128)S(1)}, u32[]{:S(2)}) copy-start(f32[32]{0:T(128)S(1)} %div.22) | copy-start | bytes 388
  385.5 101.8 %copy-start.10 = (f32[32,768]{1,0:T(8,128)}, f32[32,768]{1,0:T(8,128)S(1)}, u32[]{:S(2)}) copy-start(f32[32,768]{1,0:T(8,128)S(1)} %get-tuple-element.335) | copy-start | bytes 294916
  448.0 39.3 %copy-start.20 = (f32[32]{0:T(128)}, f32[32]{0:T(128)S(1)}, u32[]{:S(2)}) copy-start(f32[32]{0:T(128)S(1)} %psum.44) | copy-start | bytes 388
  507.1 1.9 copy-start.12
  534.4 1.9 copy-start.12
  561.8 1.9 copy-start.12
  589.2 1.9 copy-start.12
  616.6 1.9 copy-start.12
  625.8 1.7 copy-start.2
  626.8 103.1 %reduce-scatter.17.cloned.1.call-start = ((), (), s32[]{:S(2)}) async-start(), calls=%async_computation.10 | async-start | bytes 1671168 | tf_op jit(solution)/shard_map/reduce_scatter | solution.py:42
  628.8 101.2 %copy-start.3 = (f32[32,768]{1,0:T(8,128)S(1)}, f32[32,768]{1,0:T(8,128)}, u32[]{:S(2)}) copy-start(f32[32,768]{1,0:T(8,128)} %get-tuple-element.333) | copy-start | bytes 294916
  628.8 168.1 %copy-start.21 = (f32[32]{0:T(128)S(1)}, f32[32]{0:T(128)}, u32[]{:S(2)}) copy-start(f32[32]{0:T(128)} %copy-done.20) | copy-start | bytes 388
  628.8 168.1 %copy-start.11 = (f32[32,768]{1,0:T(8,128)S(1)}, f32[32,768]{1,0:T(8,128)}, u32[]{:S(2)}) copy-start(f32[32,768]{1,0:T(8,128)} %copy-done.10) | copy-start | bytes 294916
  628.8 435.7 %reduce-scatter.23.cloned.1.call-start = ((), (), s32[]{:S(2)}) async-start(), calls=%async_computation.13 | async-start | bytes 884736 | tf_op jit(solution)/shard_map/reduce_scatter | solution.py:45
  796.9 102.6 %copy-start.18 = (f32[32]{0:T(128)}, f32[32]{0:T(128)S(1)}, u32[]{:S(2)}) copy-start(f32[32]{0:T(128)S(1)} %div.24) | copy-start | bytes 388
  798.1 101.5 %copy-start.8 = (f32[32,768]{1,0:T(8,128)}, f32[32,768]{1,0:T(8,128)S(1)}, u32[]{:S(2)}) copy-start(f32[32,768]{1,0:T(8,128)S(1)} %get-tuple-element.331) | copy-start | bytes 294916
  860.6 39.0 %copy-start.22 = (f32[32]{0:T(128)}, f32[32]{0:T(128)S(1)}, u32[]{:S(2)}) copy-start(f32[32]{0:T(128)S(1)} %psum.46) | copy-start | bytes 388
  860.6 39.0 %copy-start.14 = (f32[32]{0:T(128)}, f32[32]{0:T(128)S(1)}, u32[]{:S(2)}) copy-start(f32[32]{0:T(128)S(1)} %div.25) | copy-start | bytes 388
  919.2 1.9 copy-start.13
  946.6 1.9 copy-start.13
  974.0 1.9 copy-start.13
  1001.4 1.9 copy-start.13
  1028.8 1.9 copy-start.13
  1038.0 1.7 copy-start
  1039.0 103.3 %reduce-scatter.21.cloned.1.call-start = ((), (), s32[]{:S(2)}) async-start(), calls=%async_computation.12 | async-start | bytes 1671168 | tf_op jit(solution)/shard_map/reduce_scatter | solution.py:42
  1040.9 101.4 %copy-start.4 = (f32[32,768]{1,0:T(8,128)S(1)}, f32[32,768]{1,0:T(8,128)}, u32[]{:S(2)}) copy-start(f32[32,768]{1,0:T(8,128)} %get-tuple-element.333) | copy-start | bytes 294916
  1040.9 101.4 %copy-start.9 = (f32[32,768]{1,0:T(8,128)S(1)}, f32[32,768]{1,0:T(8,128)}, u32[]{:S(2)}) copy-start(f32[32,768]{1,0:T(8,128)} %copy-done.8) | copy-start | bytes 294916
  1040.9 101.4 %copy-start.15 = (f32[32]{0:T(128)S(1)}, f32[32]{0:T(128)}, u32[]{:S(2)}) copy-start(f32[32]{0:T(128)} %copy-done.14) | copy-start | bytes 388
  1040.9 168.4 %copy-start.23 = (f32[32]{0:T(128)S(1)}, f32[32]{0:T(128)}, u32[]{:S(2)}) copy-start(f32[32]{0:T(128)} %copy-done.22) | copy-start | bytes 388
  1041.0 168.4 %copy-start.7 = (f32[32,768]{1,0:T(8,128)S(1)}, f32[32,768]{1,0:T(8,128)}, u32[]{:S(2)}) copy-start(f32[32,768]{1,0:T(8,128)} %param.15) | copy-start | bytes 294916
  1041.0 168.4 %copy-start.17 = (f32[32]{0:T(128)S(1)}, f32[32]{0:T(128)}, u32[]{:S(2)}) copy-start(f32[32]{0:T(128)} %copy-done.16) | copy-start | bytes 388
  1041.0 168.4 %copy-start.19 = (f32[32]{0:T(128)S(1)}, f32[32]{0:T(128)}, u32[]{:S(2)}) copy-start(f32[32]{0:T(128)} %copy-done.18) | copy-start | bytes 388
Sparse Core Ops, SparseCore 0:
  23.1 36.3 reduce-scatter.26
  62.9 82.0 reduce-scatter.24
  212.7 26.9 reduce-scatter.14
  242.8 74.3 reduce-scatter.12
  626.9 25.3 reduce-scatter.18
  655.4 74.4 reduce-scatter.16
  1039.1 25.3 reduce-scatter.22
  1067.7 74.5 reduce-scatter.20
where the time goes:
time: 1230 us; the launch traced here: 1220 us
  blocking collectives  439 us (36%)
  waiting for transfers between devices  303 us (25%)
  other arithmetic  297 us (24%)
  matrix products  98.6 us (8%)
  local copies, waits for them, and re-layouts  64 us (5%)
  between operations  15.1 us (1%)
    psum x5, blocking collectives, inner_sums(): return lax.psum(parts, ('row', 'col'))  323 us
    reduce_scatter x3, waiting for transfers between devices, to_rows(): lax.psum_scatter(partial_value, 'col', scatter_dimension=1, tiled=True)  233 us
    scatter-add x15, other arithmetic, one_block(): forward_sum.at[:, rows_here, :].add(forward)  177 us
    reduce_scatter x3, waiting for transfers between devices, to_cols(): lax.psum_scatter(partial_value, 'row', scatter_dimension=1, tiled=True)  69.7 us
    scatter-add x15, other arithmetic, one_block(): backward_sum.at[:, cols_here, :].add(backward)  66.7 us
    all_gather x3, blocking collectives, per_device(): graph_row_dir = lax.all_gather(graph_own_low, 'col', axis=1, tiled=True)  61.4 us
    dot_general x15, matrix products, one_block(): jnp.einsum('ksd,sod->kso', col_pieces, tiles_here, preferred_element_type...  55.3 us
    all_gather x3, blocking collectives, per_device(): graph_col_dir = lax.all_gather(graph_own_low, 'row', axis=1, tiled=True)  54.9 us
  transfers between devices with their start and end apart: 8, of which 6 were waited for; matrix products, arithmetic and copies ran while one was open for 13% of the time, Pallas kernels for 0%

commit v1 on v0

--- a/solution.py
+++ b/solution.py
@@ -1,3 +1,4 @@
+import functools
 import jax
 import jax.numpy as jnp
 from jax import lax
@@ -6,6 +7,16 @@
 PER_ROW = 5
 ITERS = 3
 coupling = 0.2
+
+
+def _direct_quarters(content, mesh_dim):
+    b_now = lax.axis_size(mesh_dim)
+    arr_next = jnp.stack([content] * b_now)
+    y = lax.all_to_all(arr_next, mesh_dim, 0, 0)
+    return jnp.concatenate(y, axis=1)
+
+
+perform_levels_all_in = functools.partial(_direct_quarters, mesh_dim="col")
 
 
 def per_device(scores, tile_values, tile_rows, tile_cols, tile_count):
@@ -56,7 +67,7 @@
     for step_index in range(ITERS):
         graph_own_low = direction.astype(jnp.bfloat16)
         graph_col_dir = lax.all_gather(graph_own_low, "row", axis=1, tiled=True)
-        graph_row_dir = lax.all_gather(graph_own_low, "col", axis=1, tiled=True)
+        graph_row_dir = perform_levels_all_in(graph_own_low)
         col_blocks = graph_col_dir.reshape(task_count, col_tiles, tile_size)
         row_blocks = graph_row_dir.reshape(task_count, row_tiles, tile_size)
         block_count = (live_count + block_slots - 1) // block_slots

time: 1230 us -> 1190 us (0.967)
  blocking collectives: 439 us -> 365 us
  starting transfers between devices: 0.33 us -> 17.7 us
    all_gather x3 -> x0, blocking collectives: 61.4 us -> none  [per_device(): graph_row_dir = lax.all_gather(graph_own_low, 'col', axis=1, tiled=True)]
    all_to_all x0 -> x3, starting transfers between devices: none -> 17.2 us  [_direct_quarters(): y = lax.all_to_all(arr_next, mesh_dim, 0, 0)]
    all_gather x3, blocking collectives: 54.9 us -> 41.7 us  [per_device(): graph_col_dir = lax.all_gather(graph_own_low, 'row', axis=1, tiled=True)]
  transfers between devices with their start and end apart: 8 -> 11, of which waited for: 6 -> 6; matrix products, arithmetic and copies ran while one was open for 13% -> 14% of each run, Pallas kernels for 0% -> 0%
where the time goes in v1:
time: 1190 us; the launch traced here: 1180 us
  blocking collectives  365 us (31%)
  waiting for transfers between devices  311 us (26%)
  other arithmetic  299 us (25%)
  matrix products  98.8 us (8%)
  local copies, waits for them, and re-layouts  69.8 us (6%)
  starting transfers between devices  17.7 us (1%)
  between operations  15.1 us (1%)
    psum x5, blocking collectives, inner_sums(): return lax.psum(parts, ('row', 'col'))  323 us
    reduce_scatter x3, waiting for transfers between devices, to_rows(): lax.psum_scatter(partial_value, 'col', scatter_dimension=1, tiled=True)  233 us
    scatter-add x15, other arithmetic, one_block(): forward_sum.at[:, rows_here, :].add(forward)  177 us
    reduce_scatter x3, waiting for transfers between devices, to_cols(): lax.psum_scatter(partial_value, 'row', scatter_dimension=1, tiled=True)  78.7 us
    scatter-add x15, other arithmetic, one_block(): backward_sum.at[:, cols_here, :].add(backward)  66.7 us
    dot_general x15, matrix products, one_block(): jnp.einsum('ksd,sod->kso', col_pieces, tiles_here, preferred_element_type...  55.4 us
    dot_general x15, matrix products, one_block(): jnp.einsum('kso,sod->ksd', row_pieces, tiles_here, preferred_element_type...  43.4 us
    all_gather x3, blocking collectives, per_device(): graph_col_dir = lax.all_gather(graph_own_low, 'row', axis=1, tiled=True)  41.7 us
  transfers between devices with their start and end apart: 11, of which 6 were waited for; matrix products, arithmetic and copies ran while one was open for 14% of the time, Pallas kernels for 0%

profile of v1, /device:TPU:1, one launch (start us, length us, event | category | flops | bytes accessed | tf_op | source)
XLA Modules:
  0.0 1177.2 jit_solution(3118179976290717480)
XLA Ops:
  9.0 8.4 all-to-all-start
  18.2 9.8 convert_reduce_fusion
  36.2 4.0 copy.54
  40.3 14.3 %all_gather.9 = bf16[32,6144]{1,0:T(8,128)(2,1)S(1)} all-gather(bf16[32,768]{1,0:T(8,128)(2,1)S(1)} %convert_element_type.43), channel_id=1, replica_groups=mesh['row'=8,'col'=16] {'row'}, dimensions={1}, use_global_device_ids=true | all-gather | bytes 442368 | tf_op jit(solution)/shard_map/all_gather | solution.py:69
  58.5 137.4 %while.36 = (s32[]{:T(128)}, f32[32,96,128]{2,0,1:T(8,128)}, f32[32,48,128]{2,0,1:T(8,128)S(1)}, s32[]{:T(128)}, s32[480]{0:T(512)}, /*index=5*/bf16[480,128,128...) while((s32[]{:T(128)}, f32[32,96,128]{2,0,1:T(8,128)}, ...), condition=%wide.region_11.14_spmd, body=%wide.region_8.13_spmd.sunk | while | flops 203689376 | bytes 23607144 | solution.py:107
  61.2 3.7 multiply_bitcast_fusion.12
  64.9 11.8 %scatter_fusion = f32[32,96,128]{2,0,1:T(8,128)} fusion(f32[32,96,128]{2,0,1:T(8,128)} %get-tuple-element.569, s32[96]{0:T(128)S(1)} %get-tuple-element.522, f32[96,32,128]{2,1,0:T(8,128)S(1)} %multiply_bitcast_fusion.12), kind=kCustom, calls=%fused_computation.6.clone.1 | custom fusion | flops 393216 | bytes 4718976 | tf_op jit(solution)/shard_map/while/body/scatter-add | solution.py:99
  81.5 4.4 scatter_fusion.1
  88.6 3.7 multiply_bitcast_fusion.12
  92.4 11.9 %scatter_fusion = f32[32,96,128]{2,0,1:T(8,128)} fusion(f32[32,96,128]{2,0,1:T(8,128)} %get-tuple-element.569, s32[96]{0:T(128)S(1)} %get-tuple-element.522, f32[96,32,128]{2,1,0:T(8,128)S(1)} %multiply_bitcast_fusion.12), kind=kCustom, calls=%fused_computation.6.clone.1 | custom fusion | flops 393216 | bytes 4718976 | tf_op jit(solution)/shard_map/while/body/scatter-add | solution.py:99
  109.1 4.5 scatter_fusion.1
  116.3 3.8 multiply_bitcast_fusion.12
  120.1 11.8 %scatter_fusion = f32[32,96,128]{2,0,1:T(8,128)} fusion(f32[32,96,128]{2,0,1:T(8,128)} %get-tuple-element.569, s32[96]{0:T(128)S(1)} %get-tuple-element.522, f32[96,32,128]{2,1,0:T(8,128)S(1)} %multiply_bitcast_fusion.12), kind=kCustom, calls=%fused_computation.6.clone.1 | custom fusion | flops 393216 | bytes 4718976 | tf_op jit(solution)/shard_map/while/body/scatter-add | solution.py:99
  136.7 4.4 scatter_fusion.1
  143.8 3.7 multiply_bitcast_fusion.12
  147.5 11.8 %scatter_fusion = f32[32,96,128]{2,0,1:T(8,128)} fusion(f32[32,96,128]{2,0,1:T(8,128)} %get-tuple-element.569, s32[96]{0:T(128)S(1)} %get-tuple-element.522, f32[96,32,128]{2,1,0:T(8,128)S(1)} %multiply_bitcast_fusion.12), kind=kCustom, calls=%fused_computation.6.clone.1 | custom fusion | flops 393216 | bytes 4718976 | tf_op jit(solution)/shard_map/while/body/scatter-add | solution.py:99
  164.1 4.4 scatter_fusion.1
  171.2 3.7 multiply_bitcast_fusion.12
  174.9 11.8 %scatter_fusion = f32[32,96,128]{2,0,1:T(8,128)} fusion(f32[32,96,128]{2,0,1:T(8,128)} %get-tuple-element.569, s32[96]{0:T(128)S(1)} %get-tuple-element.522, f32[96,32,128]{2,1,0:T(8,128)S(1)} %multiply_bitcast_fusion.12), kind=kCustom, calls=%fused_computation.6.clone.1 | custom fusion | flops 393216 | bytes 4718976 | tf_op jit(solution)/shard_map/while/body/scatter-add | solution.py:99
  191.4 4.4 scatter_fusion.1
  201.2 25.4 %reduce-scatter.15.cloned.1.call-done = f32[32,768]{1,0:T(8,128)} async-done(((f32[32,6144]{1,0:T(8,128)}), f32[32,768]{1,0:T(8,128)}) %reduce-scatter.15.cloned.1.call-update) | async-done | bytes 98320 | tf_op jit(solution)/shard_map/reduce_scatter | solution.py:56
  226.6 77.5 %reduce-scatter.13.cloned.1.call-done = f32[32,768]{1,0:T(8,128)} async-done(((f32[32,12288]{1,0:T(8,128)}), f32[32,768]{1,0:T(8,128)}) %reduce-scatter.13.cloned.1.call-update) | async-done | bytes 98320 | tf_op jit(solution)/shard_map/reduce_scatter | solution.py:53
  305.2 65.9 %all-reduce = (f32[32]{0:T(128)S(1)}, f32[32]{0:T(128)S(1)}) all-reduce(f32[32]{0:T(128)S(1)} %get-tuple-element.255, f32[32]{0:T(128)S(1)} %get-tuple-element.254), channel_id=1, replica_groups=mesh['row'=8,'col'=16] {'row','col'}, use_global_device_ids=true, to_apply=%region_1.0 | all-reduce | flops 64 | bytes 512 | tf_op jit(solution)/shard_map/psum | solution.py:61
  372.3 62.5 %psum.44 = f32[32]{0:T(128)S(1)} all-reduce(f32[32]{0:T(128)S(1)} %get-tuple-element.334), channel_id=1, replica_groups=mesh['row'=8,'col'=16] {'row','col'}, use_global_device_ids=true, to_apply=%region_17.20 | all-reduce | flops 32 | bytes 256 | tf_op jit(solution)/shard_map/psum | solution.py:61
  436.5 4.4 all-to-all-start.1
  440.9 13.7 %all_gather.10 = bf16[32,6144]{1,0:T(8,128)(2,1)S(1)} all-gather(bf16[32,768]{1,0:T(8,128)(2,1)S(1)} %get-tuple-element.332), channel_id=1, replica_groups=mesh['row'=8,'col'=16] {'row'}, dimensions={1}, use_global_device_ids=true | all-gather | bytes 442368 | tf_op jit(solution)/shard_map/all_gather | solution.py:69
  458.5 137.3 %while.37 = (s32[]{:T(128)}, f32[32,96,128]{2,0,1:T(8,128)}, f32[32,48,128]{2,0,1:T(8,128)S(1)}, s32[]{:T(128)}, s32[480]{0:T(512)}, /*index=5*/bf16[480,128,128...) while((s32[]{:T(128)}, f32[32,96,128]{2,0,1:T(8,128)}, ...), condition=%wide.region_21.24_spmd, body=%wide.region_18.23_spmd.sunk | while | flops 203689376 | bytes 23607556 | solution.py:107
  461.3 3.7 multiply_bitcast_fusion.14
  465.0 11.8 %scatter_fusion.2 = f32[32,96,128]{2,0,1:T(8,128)} fusion(f32[32,96,128]{2,0,1:T(8,128)} %get-tuple-element.611, s32[96]{0:T(128)S(1)} %get-tuple-element.536, f32[96,32,128]{2,1,0:T(8,128)S(1)} %multiply_bitcast_fusion.14), kind=kCustom, calls=%fused_computation.8.clone.1 | custom fusion | flops 393216 | bytes 4718976 | tf_op jit(solution)/shard_map/while/body/scatter-add | solution.py:99
  481.5 4.4 scatter_fusion.3
  488.7 3.7 multiply_bitcast_fusion.14
  492.4 11.8 %scatter_fusion.2 = f32[32,96,128]{2,0,1:T(8,128)} fusion(f32[32,96,128]{2,0,1:T(8,128)} %get-tuple-element.611, s32[96]{0:T(128)S(1)} %get-tuple-element.536, f32[96,32,128]{2,1,0:T(8,128)S(1)} %multiply_bitcast_fusion.14), kind=kCustom, calls=%fused_computation.8.clone.1 | custom fusion | flops 393216 | bytes 4718976 | tf_op jit(solution)/shard_map/while/body/scatter-add | solution.py:99
  509.0 4.5 scatter_fusion.3
  516.2 3.7 multiply_bitcast_fusion.14
  519.9 11.8 %scatter_fusion.2 = f32[32,96,128]{2,0,1:T(8,128)} fusion(f32[32,96,128]{2,0,1:T(8,128)} %get-tuple-element.611, s32[96]{0:T(128)S(1)} %get-tuple-element.536, f32[96,32,128]{2,1,0:T(8,128)S(1)} %multiply_bitcast_fusion.14), kind=kCustom, calls=%fused_computation.8.clone.1 | custom fusion | flops 393216 | bytes 4718976 | tf_op jit(solution)/shard_map/while/body/scatter-add | solution.py:99
  536.4 4.4 scatter_fusion.3
  543.7 3.7 multiply_bitcast_fusion.14
  547.3 11.8 %scatter_fusion.2 = f32[32,96,128]{2,0,1:T(8,128)} fusion(f32[32,96,128]{2,0,1:T(8,128)} %get-tuple-element.611, s32[96]{0:T(128)S(1)} %get-tuple-element.536, f32[96,32,128]{2,1,0:T(8,128)S(1)} %multiply_bitcast_fusion.14), kind=kCustom, calls=%fused_computation.8.clone.1 | custom fusion | flops 393216 | bytes 4718976 | tf_op jit(solution)/shard_map/while/body/scatter-add | solution.py:99
  563.9 4.4 scatter_fusion.3
  571.1 3.7 multiply_bitcast_fusion.14
  574.8 11.8 %scatter_fusion.2 = f32[32,96,128]{2,0,1:T(8,128)} fusion(f32[32,96,128]{2,0,1:T(8,128)} %get-tuple-element.611, s32[96]{0:T(128)S(1)} %get-tuple-element.536, f32[96,32,128]{2,1,0:T(8,128)S(1)} %multiply_bitcast_fusion.14), kind=kCustom, calls=%fused_computation.8.clone.1 | custom fusion | flops 393216 | bytes 4718976 | tf_op jit(solution)/shard_map/while/body/scatter-add | solution.py:99
  591.3 4.4 scatter_fusion.3
  598.8 26.7 %reduce-scatter.19.cloned.1.call-done = f32[32,768]{1,0:T(8,128)} async-done(((f32[32,6144]{1,0:T(8,128)}), f32[32,768]{1,0:T(8,128)}) %reduce-scatter.19.cloned.1.call-update) | async-done | bytes 98320 | tf_op jit(solution)/shard_map/reduce_scatter | solution.py:56
  625.5 77.5 %reduce-scatter.17.cloned.1.call-done = f32[32,768]{1,0:T(8,128)} async-done(((f32[32,12288]{1,0:T(8,128)}), f32[32,768]{1,0:T(8,128)}) %reduce-scatter.17.cloned.1.call-update) | async-done | bytes 98320 | tf_op jit(solution)/shard_map/reduce_scatter | solution.py:53
  704.1 65.9 %psum.45 = f32[32]{0:T(128)S(1)} all-reduce(f32[32]{0:T(128)S(1)} %multiply_reduce_fusion.2), channel_id=1, replica_groups=mesh['row'=8,'col'=16] {'row','col'}, use_global_device_ids=true, to_apply=%region_25.28 | all-reduce | flops 32 | bytes 256 | tf_op jit(solution)/shard_map/psum | solution.py:61
  771.1 62.7 %psum.46 = f32[32]{0:T(128)S(1)} all-reduce(f32[32]{0:T(128)S(1)} %get-tuple-element.330), channel_id=1, replica_groups=mesh['row'=8,'col'=16] {'row','col'}, use_global_device_ids=true, to_apply=%region_27.30 | all-reduce | flops 32 | bytes 256 | tf_op jit(solution)/shard_map/psum | solution.py:61
  834.9 4.4 all-to-all-start.2
  839.4 13.7 %all_gather.11 = bf16[32,6144]{1,0:T(8,128)(2,1)S(1)} all-gather(bf16[32,768]{1,0:T(8,128)(2,1)S(1)} %fusion.69), channel_id=1, replica_groups=mesh['row'=8,'col'=16] {'row'}, dimensions={1}, use_global_device_ids=true | all-gather | bytes 442368 | tf_op jit(solution)/shard_map/all_gather | solution.py:69
  857.0 137.3 %while.38 = (s32[]{:T(128)}, f32[32,96,128]{2,0,1:T(8,128)}, f32[32,48,128]{2,0,1:T(8,128)S(1)}, s32[]{:T(128)}, s32[480]{0:T(512)}, /*index=5*/bf16[480,128,128...) while((s32[]{:T(128)}, f32[32,96,128]{2,0,1:T(8,128)}, ...), condition=%wide.region_31.34_spmd, body=%wide.region_28.33_spmd.sunk | while | flops 203689376 | bytes 23607556 | solution.py:107
  859.7 3.7 multiply_bitcast_fusion.16
  863.4 11.8 %scatter_fusion.4 = f32[32,96,128]{2,0,1:T(8,128)} fusion(f32[32,96,128]{2,0,1:T(8,128)} %get-tuple-element.653, s32[96]{0:T(128)S(1)} %get-tuple-element.550, f32[96,32,128]{2,1,0:T(8,128)S(1)} %multiply_bitcast_fusion.16), kind=kCustom, calls=%fused_computation.10.clone.1 | custom fusion | flops 393216 | bytes 4718976 | tf_op jit(solution)/shard_map/while/body/scatter-add | solution.py:99
  880.0 4.4 scatter_fusion.5
  890.9 11.8 %scatter_fusion.4 = f32[32,96,128]{2,0,1:T(8,128)} fusion(f32[32,96,128]{2,0,1:T(8,128)} %get-tuple-element.653, s32[96]{0:T(128)S(1)} %get-tuple-element.550, f32[96,32,128]{2,1,0:T(8,128)S(1)} %multiply_bitcast_fusion.16), kind=kCustom, calls=%fused_computation.10.clone.1 | custom fusion | flops 393216 | bytes 4718976 | tf_op jit(solution)/shard_map/while/body/scatter-add | solution.py:99
  907.4 4.5 scatter_fusion.5
  914.7 3.7 multiply_bitcast_fusion.16
  918.3 11.8 %scatter_fusion.4 = f32[32,96,128]{2,0,1:T(8,128)} fusion(f32[32,96,128]{2,0,1:T(8,128)} %get-tuple-element.653, s32[96]{0:T(128)S(1)} %get-tuple-element.550, f32[96,32,128]{2,1,0:T(8,128)S(1)} %multiply_bitcast_fusion.16), kind=kCustom, calls=%fused_computation.10.clone.1 | custom fusion | flops 393216 | bytes 4718976 | tf_op jit(solution)/shard_map/while/body/scatter-add | solution.py:99
  934.9 4.4 scatter_fusion.5
  945.8 11.8 %scatter_fusion.4 = f32[32,96,128]{2,0,1:T(8,128)} fusion(f32[32,96,128]{2,0,1:T(8,128)} %get-tuple-element.653, s32[96]{0:T(128)S(1)} %get-tuple-element.550, f32[96,32,128]{2,1,0:T(8,128)S(1)} %multiply_bitcast_fusion.16), kind=kCustom, calls=%fused_computation.10.clone.1 | custom fusion | flops 393216 | bytes 4718976 | tf_op jit(solution)/shard_map/while/body/scatter-add | solution.py:99
  962.3 4.4 scatter_fusion.5
  973.2 11.8 %scatter_fusion.4 = f32[32,96,128]{2,0,1:T(8,128)} fusion(f32[32,96,128]{2,0,1:T(8,128)} %get-tuple-element.653, s32[96]{0:T(128)S(1)} %get-tuple-element.550, f32[96,32,128]{2,1,0:T(8,128)S(1)} %multiply_bitcast_fusion.16), kind=kCustom, calls=%fused_computation.10.clone.1 | custom fusion | flops 393216 | bytes 4718976 | tf_op jit(solution)/shard_map/while/body/scatter-add | solution.py:99
  989.8 4.4 scatter_fusion.5
  997.3 26.6 %reduce-scatter.23.cloned.1.call-done = f32[32,768]{1,0:T(8,128)} async-done(((f32[32,6144]{1,0:T(8,128)}), f32[32,768]{1,0:T(8,128)}) %reduce-scatter.23.cloned.1.call-update) | async-done | bytes 98320 | tf_op jit(solution)/shard_map/reduce_scatter | solution.py:56
  1023.9 77.6 %reduce-scatter.21.cloned.1.call-done = f32[32,768]{1,0:T(8,128)} async-done(((f32[32,12288]{1,0:T(8,128)}), f32[32,768]{1,0:T(8,128)}) %reduce-scatter.21.cloned.1.call-update) | async-done | bytes 98320 | tf_op jit(solution)/shard_map/reduce_scatter | solution.py:53
  1102.7 65.9 %psum.47 = f32[32]{0:T(128)S(1)} all-reduce(f32[32]{0:T(128)S(1)} %multiply_reduce_fusion), channel_id=1, replica_groups=mesh['row'=8,'col'=16] {'row','col'}, use_global_device_ids=true, to_apply=%region_35.38 | all-reduce | flops 32 | bytes 256 | tf_op jit(solution)/shard_map/psum | solution.py:61
  (241 shorter events, 166.0 us)
Async XLA Ops:
  9.0 45.7 %all-to-all-start = ((bf16[16,32,768]{2,1,0:T(8,128)(2,1)}), bf16[16,32,768]{2,1,0:T(8,128)(2,1)S(1)}, u32[]{:S(2)}, u32[]{:S(2)}) async-start(bf16[16,32,768]{2,1,0:T(8,128)(2,1)} %stack.6), calls=%async_computation | async-start | bytes 1572864 | tf_op jit(solution)/shard_map/all_to_all | solution.py:15
  17.5 181.5 %reduce-scatter.27.cloned.1.call-start = ((), (), s32[]{:S(2)}) async-start(), calls=%async_computation.18 | async-start | bytes 3538944
  33.2 166.8 %reduce-scatter.25.cloned.1.call-start = ((), (), s32[]{:S(2)}) async-start(), calls=%async_computation.17 | async-start | bytes 6684672
  40.3 186.4 %reduce-scatter.15.cloned.1.call-start = ((), (), s32[]{:S(2)}) async-start(), calls=%async_computation.12 | async-start | bytes 884736 | tf_op jit(solution)/shard_map/reduce_scatter | solution.py:56
  195.9 1.7 copy-start.1
  196.9 107.2 %reduce-scatter.13.cloned.1.call-start = ((), (), s32[]{:S(2)}) async-start(), calls=%async_computation.11 | async-start | bytes 1671168 | tf_op jit(solution)/shard_map/reduce_scatter | solution.py:53
  198.9 105.3 %copy-start.5 = (f32[32,768]{1,0:T(8,128)S(1)}, f32[32,768]{1,0:T(8,128)}, u32[]{:S(2)}) copy-start(f32[32,768]{1,0:T(8,128)} %param.15) | copy-start | bytes 294916
  371.1 65.3 %copy-start.15 = (f32[32]{0:T(128)}, f32[32]{0:T(128)S(1)}, u32[]{:S(2)}) copy-start(f32[32]{0:T(128)S(1)} %div.22) | copy-start | bytes 388
  372.3 64.2 %copy-start.9 = (f32[32,768]{1,0:T(8,128)}, f32[32,768]{1,0:T(8,128)S(1)}, u32[]{:S(2)}) copy-start(f32[32,768]{1,0:T(8,128)S(1)} %get-tuple-element.335) | copy-start | bytes 294916
  434.8 1.7 copy-start.19
  436.5 18.3 %all-to-all-start.1 = ((bf16[16,32,768]{2,1,0:T(8,128)(2,1)}), bf16[16,32,768]{2,1,0:T(8,128)(2,1)S(1)}, u32[]{:S(2)}, u32[]{:S(2)}) async-start(bf16[16,32,768]{2,1,0:T(8,128)(2,1)} %stack.7), calls=%async_computation.3 | async-start | bytes 1572864 | tf_op jit(solution)/shard_map/all_to_all | solution.py:15
  440.9 184.6 %reduce-scatter.19.cloned.1.call-start = ((), (), s32[]{:S(2)}) async-start(), calls=%async_computation.14 | async-start | bytes 884736 | tf_op jit(solution)/shard_map/reduce_scatter | solution.py:56
  476.8 1.9 copy-start.11
  504.2 1.9 copy-start.11
  531.7 1.9 copy-start.11
  559.1 1.9 copy-start.11
  586.6 1.9 copy-start.11
  595.8 1.7 copy-start.2
  596.8 106.2 %reduce-scatter.17.cloned.1.call-start = ((), (), s32[]{:S(2)}) async-start(), calls=%async_computation.13 | async-start | bytes 1671168 | tf_op jit(solution)/shard_map/reduce_scatter | solution.py:53
  598.8 104.2 %copy-start.3 = (f32[32,768]{1,0:T(8,128)S(1)}, f32[32,768]{1,0:T(8,128)}, u32[]{:S(2)}) copy-start(f32[32,768]{1,0:T(8,128)} %get-tuple-element.333) | copy-start | bytes 294916
  598.8 171.2 %copy-start.20 = (f32[32]{0:T(128)S(1)}, f32[32]{0:T(128)}, u32[]{:S(2)}) copy-start(f32[32]{0:T(128)} %copy-done.19) | copy-start | bytes 388
  598.8 171.2 %copy-start.10 = (f32[32,768]{1,0:T(8,128)S(1)}, f32[32,768]{1,0:T(8,128)}, u32[]{:S(2)}) copy-start(f32[32,768]{1,0:T(8,128)} %copy-done.9) | copy-start | bytes 294916
  770.0 64.9 %copy-start.17 = (f32[32]{0:T(128)}, f32[32]{0:T(128)S(1)}, u32[]{:S(2)}) copy-start(f32[32]{0:T(128)S(1)} %div.24) | copy-start | bytes 388
  771.1 63.8 %copy-start.7 = (f32[32,768]{1,0:T(8,128)}, f32[32,768]{1,0:T(8,128)S(1)}, u32[]{:S(2)}) copy-start(f32[32,768]{1,0:T(8,128)S(1)} %get-tuple-element.331) | copy-start | bytes 294916
  833.9 1.1 copy-start.21
  833.9 1.1 copy-start.13
  834.9 18.3 %all-to-all-start.2 = ((bf16[16,32,768]{2,1,0:T(8,128)(2,1)}), bf16[16,32,768]{2,1,0:T(8,128)(2,1)S(1)}, u32[]{:S(2)}, u32[]{:S(2)}) async-start(bf16[16,32,768]{2,1,0:T(8,128)(2,1)} %stack.8), calls=%async_computation.6 | async-start | bytes 1572864 | tf_op jit(solution)/shard_map/all_to_all | solution.py:15
  839.3 184.6 %reduce-scatter.23.cloned.1.call-start = ((), (), s32[]{:S(2)}) async-start(), calls=%async_computation.16 | async-start | bytes 884736 | tf_op jit(solution)/shard_map/reduce_scatter | solution.py:56
  875.2 1.9 copy-start.12
  902.7 1.9 copy-start.12
  930.1 1.9 copy-start.12
  957.6 1.9 copy-start.12
  985.0 1.9 copy-start.12
  994.3 1.7 copy-start
  995.2 106.3 %reduce-scatter.21.cloned.1.call-start = ((), (), s32[]{:S(2)}) async-start(), calls=%async_computation.15 | async-start | bytes 1671168 | tf_op jit(solution)/shard_map/reduce_scatter | solution.py:53
  997.2 104.3 %copy-start.4 = (f32[32,768]{1,0:T(8,128)S(1)}, f32[32,768]{1,0:T(8,128)}, u32[]{:S(2)}) copy-start(f32[32,768]{1,0:T(8,128)} %get-tuple-element.333) | copy-start | bytes 294916
  997.2 104.3 %copy-start.8 = (f32[32,768]{1,0:T(8,128)S(1)}, f32[32,768]{1,0:T(8,128)}, u32[]{:S(2)}) copy-start(f32[32,768]{1,0:T(8,128)} %copy-done.7) | copy-start | bytes 294916
  997.2 104.3 %copy-start.14 = (f32[32]{0:T(128)S(1)}, f32[32]{0:T(128)}, u32[]{:S(2)}) copy-start(f32[32]{0:T(128)} %copy-done.13) | copy-start | bytes 388
  997.2 171.4 %copy-start.22 = (f32[32]{0:T(128)S(1)}, f32[32]{0:T(128)}, u32[]{:S(2)}) copy-start(f32[32]{0:T(128)} %copy-done.21) | copy-start | bytes 388
  997.2 171.4 %copy-start.6 = (f32[32,768]{1,0:T(8,128)S(1)}, f32[32,768]{1,0:T(8,128)}, u32[]{:S(2)}) copy-start(f32[32,768]{1,0:T(8,128)} %param.15) | copy-start | bytes 294916
  997.2 171.4 %copy-start.16 = (f32[32]{0:T(128)S(1)}, f32[32]{0:T(128)}, u32[]{:S(2)}) copy-start(f32[32]{0:T(128)} %copy-done.15) | copy-start | bytes 388
  997.2 171.4 %copy-start.18 = (f32[32]{0:T(128)S(1)}, f32[32]{0:T(128)}, u32[]{:S(2)}) copy-start(f32[32]{0:T(128)} %copy-done.17) | copy-start | bytes 388
Sparse Core Ops, SparseCore 0:
  33.3 35.8 reduce-scatter.26
  72.7 81.7 reduce-scatter.24
  197.0 29.5 reduce-scatter.14
  229.7 74.3 reduce-scatter.12
  596.9 28.5 reduce-scatter.18
  628.6 74.3 reduce-scatter.16
  995.4 28.4 reduce-scatter.22
  1027.1 74.3 reduce-scatter.20
